TPU v7x, 256 devices: a whole 4x4x8 slice. The times are simulated.
256 devices in a mesh: row: 32 (over x, y, core), col: 8 (over z).
Axes of the slice: x: 4, y: 4, z: 8, core: 2. Of those that a mesh axis runs over, the one named last changes fastest.
Arguments:
- rhs: float32 [4, 2048, 1024], P(None, 'row', 'col'), may hold values from -6 to 6
- l_panel: bfloat16 [4, 2048, 32768], P(None, 'row', 'col'), may hold values from -0.03125 to 0.03125
- x_solved: bfloat16 [32768, 1024], P('col'), may hold values from -6 to 6
- diag_inv: bfloat16 [4, 2048, 2048], P(None, 'row'), may hold values from -1 to 1.5, as said below
- l_inner: bfloat16 [6, 2048, 2048], P(None, 'row'), may hold values from -0.0625 to 0.0625
Outputs:
- x_window: float32 [4, 2048, 1024], P(None, 'row', 'col')
Inputs may be any that keep to these rules, and one draw needn't show every extreme that they name: `diag_inv`: each block is lower triangular with diagonal entries between one half and three halves.
All inputs are finite; a program needn't handle non-finite values.
Results may differ from a plain program's by a relative error of at most 0.0045.
Values may be sent and summed in bfloat16 or wider, within the bound.
A program may use at most 64 MiB of HBM per device.

v0:
```python
import jax
import jax.numpy as jnp
from jax import lax
from jax.sharding import PartitionSpec as P


def cut_along(x, dim, count):
    before, after = (x.shape[:dim], x.shape[dim + 1 :])
    return jnp.moveaxis(x.reshape(*before, count, -1, *after), dim, 0)


def sent_and_summed(x, axis, dim):
    blocks = cut_along(x, dim, lax.axis_size(axis))
    arrived = lax.all_to_all(blocks, axis, split_axis=0, concat_axis=0, tiled=True)
    return arrived.sum(axis=0)


def sent_to_all(x, axis):
    copies = jnp.broadcast_to(x, (lax.axis_size(axis), *x.shape))
    return lax.all_to_all(copies, axis, split_axis=0, concat_axis=0, tiled=True)


def in_order(blocks, dim):
    dims = list(blocks.shape[1:])
    dims[dim] *= blocks.shape[0]
    return jnp.moveaxis(blocks, 0, dim).reshape(dims)


def collect(x, axis, dim):
    blocks = sent_to_all(x, axis)
    return in_order(blocks, dim)


def inner_index(target, earlier):
    return target * (target - 1) // 2 + earlier


def local(rhs, l_panel, x_solved, diag_inv, l_inner):
    step_count, local_rows, solved_count = l_panel.shape
    local_width = rhs.shape[2]
    reduced = []
    products = jnp.dot(
        l_panel.reshape(step_count * local_rows, solved_count),
        x_solved,
        preferred_element_type=jnp.float32,
    )
    products = products.reshape(step_count, local_rows, x_solved.shape[1])
    shares = sent_and_summed(products, "col", 2)
    for target in range(step_count):
        reduced.append(rhs[target] - shares[target])
    empty = jnp.zeros((local_rows, local_width), jnp.float32)
    results = []
    pending = list(reduced)
    for target in range(step_count):
        resid = pending[target]
        resid_low = resid.astype(jnp.bfloat16)
        apply_columns = diag_inv[target]
        current = jnp.dot(
            apply_columns, collect(resid_low, "row", 0), preferred_element_type=jnp.float32
        )
        results.append(current)
        if target + 1 < step_count:
            current_low = current.astype(jnp.bfloat16)
            later = tuple(range(target + 1, step_count))

            def subtract_later(carried, segment, offset, target=target, later=later):
                updated = []
                for position, follower in enumerate(later):
                    columns = l_inner[inner_index(follower, target)]
                    updated.append(jnp.dot(columns, segment, preferred_element_type=jnp.float32))
                return tuple(updated)

            updates = subtract_later(
                tuple((empty for follower in later)), collect(current_low, "row", 0), jnp.int32(0)
            )
            for position, follower in enumerate(later):
                pending[follower] = pending[follower] - updates[position]
    return jnp.stack(results, axis=0)


def solution(mesh):
    in_specs = (
        P(None, "row", "col"),
        P(None, "row", "col"),
        P("col", None),
        P(None, "row", None),
        P(None, "row", None),
    )
    out_specs = P(None, "row", "col")
    return jax.shard_map(local, mesh=mesh, in_specs=in_specs, out_specs=out_specs, check_vma=False)
```

profile of v0, /device:TPU:1, one launch (start us, length us, event | category | flops | bytes accessed | tf_op | source)
XLA Modules:
  0.0 174.1 jit_solution(17436873167216978317)
XLA Ops:
  0.0 0.0 copy-start
  0.0 11.4 %copy.10 = bf16[1024,4096]{1,0:T(8,128)(2,1)} copy(bf16[1024,4096]{0,1:T(8,128)(2,1)} %bitcast.130) | data formatting | bytes 16777216 | tf_op jit(solution)/shard_map/dot_general | solution.py:42
  11.4 0.0 copy-done
  11.4 4.8 %fusion.2 = f32[8,4,64,128]{3,2,0,1:T(8,128)S(1)} fusion(bf16[8,128,4096,1]{2,1,0,3:T(8,128)(2,1)} %bitcast.131, bf16[4,64,4096]{2,1,0:T(8,128)(2,1)S(1)} %copy-done), kind=kOutput, calls=%fused_computation.2 | convolution fusion | flops 2147483648 | bytes 11534336 | tf_op jit(solution)/shard_map/dot_general | solution.py:42
  16.2 0.1 copy.8
  16.3 0.0 copy-start.2
  16.3 36.3 %all_to_all.40 = f32[8,4,64,128]{3,2,1,0:T(8,128)S(1)} all-to-all(f32[8,4,64,128]{3,2,1,0:T(8,128)S(1)} %copy.8), channel_id=1, replica_groups=mesh['row'=32,'col'=8] {'col'}, dimensions={0} | all-to-all | bytes 2097152 | tf_op jit(solution)/shard_map/all_to_all | solution.py:14
  52.6 0.1 reduce_sum.9
  52.7 0.0 copy-done.2
  52.7 0.0 copy-start.1
  52.7 0.1 broadcast_in_dim.21
  52.8 20.9 %all_to_all.41 = bf16[32,64,128]{2,1,0:T(8,128)(2,1)S(1)} all-to-all(bf16[32,64,128]{2,1,0:T(8,128)(2,1)S(1)} %broadcast_in_dim.21), channel_id=1, replica_groups=mesh['row'=32,'col'=8] {'row'}, dimensions={0} | all-to-all | bytes 1048576 | tf_op jit(solution)/shard_map/all_to_all | solution.py:20
  73.7 0.0 copy-done.1
  73.7 0.2 bitcast_convert_fusion.2
  74.0 0.1 broadcast_in_dim.22
  74.1 15.0 %all_to_all.42 = bf16[32,64,128]{2,1,0:T(8,128)(2,1)S(1)} all-to-all(bf16[32,64,128]{2,1,0:T(8,128)(2,1)S(1)} %broadcast_in_dim.22), channel_id=1, replica_groups=mesh['row'=32,'col'=8] {'row'}, dimensions={0} | all-to-all | bytes 1048576 | tf_op jit(solution)/shard_map/all_to_all | solution.py:20
  89.1 1.2 fusion.11
  90.3 0.1 broadcast_in_dim.23
  90.4 15.0 %all_to_all.43 = bf16[32,64,128]{2,1,0:T(8,128)(2,1)S(1)} all-to-all(bf16[32,64,128]{2,1,0:T(8,128)(2,1)S(1)} %broadcast_in_dim.23), channel_id=1, replica_groups=mesh['row'=32,'col'=8] {'row'}, dimensions={0} | all-to-all | bytes 1048576 | tf_op jit(solution)/shard_map/all_to_all | solution.py:20
  105.4 0.2 bitcast_convert_fusion.1
  105.6 0.9 broadcast_in_dim.24
  106.5 3.7 %all-to-all-start.4 = ((bf16[32,64,128]{2,1,0:T(8,128)(2,1)}), bf16[32,64,128]{2,1,0:T(8,128)(2,1)S(1)}, u32[]{:S(2)}, u32[]{:S(2)}) async-start(bf16[32,64,128]{2,1,0:T(8,128)(2,1)} %broadcast_in_dim.24), calls=%async_computation.4 | async-start | bytes 1048576 | tf_op jit(solution)/shard_map/all_to_all | solution.py:20
  110.2 1.2 fusion.9
  111.4 10.4 %all-to-all-done.4 = bf16[32,64,128]{2,1,0:T(8,128)(2,1)S(1)} async-done(((bf16[32,64,128]{2,1,0:T(8,128)(2,1)}), bf16[32,64,128]{2,1,0:T(8,128)(2,1)S(1)}, u32[]{:S(2)}, u32[]{:S(2)}) %all-to-all-start.4) | async-done | bytes 524320 | tf_op jit(solution)/shard_map/all_to_all | solution.py:20
  121.8 1.2 fusion.12
  122.9 0.1 broadcast_in_dim.25
  123.1 15.0 %all_to_all.44 = bf16[32,64,128]{2,1,0:T(8,128)(2,1)S(1)} all-to-all(bf16[32,64,128]{2,1,0:T(8,128)(2,1)S(1)} %broadcast_in_dim.25), channel_id=1, replica_groups=mesh['row'=32,'col'=8] {'row'}, dimensions={0} | all-to-all | bytes 1048576 | tf_op jit(solution)/shard_map/all_to_all | solution.py:20
  138.1 1.2 bitcast_convert_fusion
  139.3 0.9 broadcast_in_dim.26
  140.2 4.4 %all-to-all-start.6 = ((bf16[32,64,128]{2,1,0:T(8,128)(2,1)}), bf16[32,64,128]{2,1,0:T(8,128)(2,1)}, u32[]{:S(2)}, u32[]{:S(2)}) async-start(bf16[32,64,128]{2,1,0:T(8,128)(2,1)} %broadcast_in_dim.26), calls=%async_computation.6 | async-start | bytes 1048576 | tf_op jit(solution)/shard_map/all_to_all | solution.py:20
  144.6 1.2 fusion.7
  145.7 1.2 fusion.6
  146.9 8.9 %all-to-all-done.6 = bf16[32,64,128]{2,1,0:T(8,128)(2,1)} async-done(((bf16[32,64,128]{2,1,0:T(8,128)(2,1)}), bf16[32,64,128]{2,1,0:T(8,128)(2,1)}, u32[]{:S(2)}, u32[]{:S(2)}) %all-to-all-start.6) | async-done | bytes 524320 | tf_op jit(solution)/shard_map/all_to_all | solution.py:20
  155.8 1.3 fusion.13
  157.2 0.1 broadcast_in_dim.27
  157.3 15.0 %all_to_all.45 = bf16[32,64,128]{2,1,0:T(8,128)(2,1)S(1)} all-to-all(bf16[32,64,128]{2,1,0:T(8,128)(2,1)S(1)} %broadcast_in_dim.27), channel_id=1, replica_groups=mesh['row'=32,'col'=8] {'row'}, dimensions={0} | all-to-all | bytes 1048576 | tf_op jit(solution)/shard_map/all_to_all | solution.py:20
  172.3 1.2 convolution_bitcast_fusion
  173.5 0.7 pad_maximum_fusion
  (1 shorter events, 0.0 us)
Async XLA Ops:
  0.0 11.4 %copy-start = (bf16[4,64,4096]{2,1,0:T(8,128)(2,1)S(1)}, bf16[4,64,4096]{2,1,0:T(8,128)(2,1)}, u32[]{:S(2)}) copy-start(bf16[4,64,4096]{2,1,0:T(8,128)(2,1)} %param.6) | copy-start | bytes 6291460
  16.3 36.4 %copy-start.2 = (f32[4,64,128]{2,1,0:T(8,128)S(1)}, f32[4,64,128]{2,1,0:T(8,128)}, u32[]{:S(2)}) copy-start(f32[4,64,128]{2,1,0:T(8,128)} %param.5) | copy-start | bytes 393220
  52.7 21.1 %copy-start.1 = (bf16[4,64,2048]{2,1,0:T(8,128)(2,1)S(1)}, bf16[4,64,2048]{2,1,0:T(8,128)(2,1)}, u32[]{:S(2)}) copy-start(bf16[4,64,2048]{2,1,0:T(8,128)(2,1)} %param.8) | copy-start | bytes 3145732
  106.5 15.2 %all-to-all-start.4 = ((bf16[32,64,128]{2,1,0:T(8,128)(2,1)}), bf16[32,64,128]{2,1,0:T(8,128)(2,1)S(1)}, u32[]{:S(2)}, u32[]{:S(2)}) async-start(bf16[32,64,128]{2,1,0:T(8,128)(2,1)} %broadcast_in_dim.24), calls=%async_computation.4 | async-start | bytes 1048576 | tf_op jit(solution)/shard_map/all_to_all | solution.py:20
  140.2 15.7 %all-to-all-start.6 = ((bf16[32,64,128]{2,1,0:T(8,128)(2,1)}), bf16[32,64,128]{2,1,0:T(8,128)(2,1)}, u32[]{:S(2)}, u32[]{:S(2)}) async-start(bf16[32,64,128]{2,1,0:T(8,128)(2,1)} %broadcast_in_dim.26), calls=%async_computation.6 | async-start | bytes 1048576 | tf_op jit(solution)/shard_map/all_to_all | solution.py:20
where the time goes:
time: 175 us; the launch traced here: 174 us
  blocking collectives  117 us (67%)
  waiting for transfers between devices  19.3 us (11%)
  matrix products  14.8 us (8%)
  local copies, waits for them, and re-layouts  13.9 us (8%)
  starting transfers between devices  8.07 us (5%)
    all_to_all x5, blocking collectives, sent_to_all(): return lax.all_to_all(copies, axis, split_axis=0, concat_axis=0, tiled=True)  81 us
    all_to_all x1, blocking collectives, sent_and_summed(): lax.all_to_all(blocks, axis, split_axis=0, concat_axis=0, tiled=True)  36.3 us
    all_to_all x2, waiting for transfers between devices, sent_to_all(): return lax.all_to_all(copies, axis, split_axis=0, concat_axis=0, tiled=True)  19.3 us
    dot_general x1, local copies, waits for them, and re-layouts, local(): jnp.dot(l_panel.reshape(step_count * local_rows, solved_count), x_solved,...  11.4 us
    all_to_all x2, starting transfers between devices, sent_to_all(): return lax.all_to_all(copies, axis, split_axis=0, concat_axis=0, tiled=True)  8.07 us
    dot_general x6, matrix products, subtract_later(): jnp.dot(columns, segment, preferred_element_type=jnp.float32)  7.19 us
    dot_general x1, matrix products, local(): jnp.dot(l_panel.reshape(step_count * local_rows, solved_count), x_solved,...  4.8 us
  transfers between devices with their start and end apart: 2, of which 2 were waited for; matrix products, arithmetic and copies ran while one was open for 2% of the time, Pallas kernels for 0%

commit v1 on v0

v1 whole, which is shorter than its diff:
```python
import jax
import jax.numpy as jnp
from jax import lax
from jax.experimental import pallas as pl
from jax.experimental.pallas import tpu as pltpu
from jax.sharding import PartitionSpec as P

MESH = pl.DeviceIdType.MESH
BF = jnp.bfloat16
F32 = jnp.float32


def dot(a, b):
    return jnp.dot(a, b, preferred_element_type=F32)


def inner_index(target, earlier):
    return target * (target - 1) // 2 + earlier


PLANE = sorted(
    [
        (min(dx, 4 - dx) + min(dy, 4 - dy), dx, dy, dc)
        for dx in range(4)
        for dy in range(4)
        for dc in range(2)
        if (dx, dy, dc) != (0, 0, 0)
    ],
    reverse=True,
)


def kernel(rhs, panel, solved, dinv, inner, out, lp, xs, dv, lv, rv, own, part, rs, g, pend,
           in_sem, rs_send, rs_recv, g_send, g_recv):
    r = lax.axis_index("row")
    c = lax.axis_index("col")
    core = r % 2
    y = (r // 2) % 4
    x = r // 8

    loads = [pltpu.make_async_copy(panel, lp, in_sem.at[0])]
    for i in range(4):
        for half, off in enumerate((4 + i, 3 - i)):
            dest = (c + off) % 8
            loads.append(
                pltpu.make_async_copy(
                    solved.at[:, pl.ds(pl.multiple_of(dest * 128, 128), 128)],
                    xs.at[i, :, pl.ds(128 * half, 128)],
                    in_sem.at[1 + 2 * i + half],
                )
            )
    loads.append(pltpu.make_async_copy(rhs, rv, in_sem.at[9]))
    loads.append(pltpu.make_async_copy(dinv, dv, in_sem.at[10]))
    loads.append(pltpu.make_async_copy(inner, lv, in_sem.at[11]))
    for cp in loads:
        cp.start()

    targets = []
    for _, dx, dy, dc in PLANE:
        targets.append((((x + dx) % 4) * 4 + (y + dy) % 4) * 2 + (core + dc) % 2)

    barrier = pltpu.get_barrier_semaphore()
    for off in range(1, 8):
        pl.semaphore_signal(barrier, inc=1, device_id=(r, (c + off) % 8), device_id_type=MESH)
    for t in targets:
        pl.semaphore_signal(barrier, inc=1, device_id=(t, c), device_id_type=MESH)

    def rs_copy(off, m):
        return pltpu.make_async_remote_copy(
            src_ref=part.at[off, m],
            dst_ref=rs.at[m, off - 1],
            send_sem=rs_send,
            recv_sem=rs_recv.at[m],
            device_id=(r, (c + off) % 8),
            device_id_type=MESH,
        )

    loads[0].wait()
    for i in range(4):
        loads[1 + 2 * i].wait()
        loads[2 + 2 * i].wait()
        acc = dot(lp[...].reshape(256, 4096), xs[i]).reshape(4, 64, 256)
        part[4 + i] = acc[:, :, :128].astype(BF)
        if i < 3:
            part[3 - i] = acc[:, :, 128:].astype(BF)
        else:
            own[...] = acc[:, :, 128:]
        if i == 0:
            pl.semaphore_wait(barrier, 38)
        rs_copy(4 + i, 0).start()
        if i < 3:
            rs_copy(3 - i, 0).start()
    for m in range(1, 4):
        for off in (4, 5, 3, 6, 2, 7, 1):
            rs_copy(off, m).start()

    mine = pl.ds(pl.multiple_of(r * 64, 64), 64)

    def reduce(m):
        pltpu.make_async_copy(rs.at[m], rs.at[m], rs_recv.at[m]).wait()
        total = own[m]
        for s in range(7):
            total = total + rs[m, s].astype(F32)
        return rv[m] - total

    def spread(n, value):
        g[n, mine, :] = value.astype(BF)
        for t in targets:
            pltpu.make_async_remote_copy(
                src_ref=g.at[n, mine],
                dst_ref=g.at[n, mine],
                send_sem=g_send.at[n],
                recv_sem=g_recv.at[n],
                device_id=(t, c),
                device_id_type=MESH,
            ).start()

    def arrived(n):
        pltpu.make_async_copy(
            g.at[n, pl.ds(0, 1984)], g.at[n, pl.ds(0, 1984)], g_recv.at[n]
        ).wait()

    loads[9].wait()
    resid = reduce(0)
    later = []
    for m in range(4):
        spread(2 * m if m < 3 else 6, resid)
        if m == 0:
            loads[10].wait()
            loads[11].wait()
            for k in range(1, 4):
                pend[k] = reduce(k)
        for target, n in later:
            pend[target] = pend[target] - dot(lv[inner_index(target, m - 1)], g[n])
        later = []
        arrived(2 * m)
        cur = dot(dv[m], g[2 * m])
        if m < 3:
            spread(2 * m + 1, cur)
        out[m] = cur
        if m < 3:
            arrived(2 * m + 1)
            resid = pend[m + 1] - dot(lv[inner_index(m + 1, m)], g[2 * m + 1])
            later = [(k, 2 * m + 1) for k in range(m + 2, 4)]

    pltpu.make_async_copy(part.at[pl.ds(1, 7)], part.at[pl.ds(1, 7)], rs_send).wait()
    for n in range(7):
        pltpu.make_async_copy(
            g.at[n, pl.ds(0, 1984)], g.at[n, pl.ds(0, 1984)], g_send.at[n]
        ).wait()


def local(rhs, l_panel, x_solved, diag_inv, l_inner):
    any_spec = pl.BlockSpec(memory_space=pl.ANY)
    return pl.pallas_call(
        kernel,
        out_shape=jax.ShapeDtypeStruct((4, 64, 128), F32),
        in_specs=[any_spec] * 5,
        out_specs=pl.BlockSpec(memory_space=pltpu.VMEM),
        scratch_shapes=[
            pltpu.VMEM((4, 64, 4096), BF),
            pltpu.VMEM((4, 4096, 256), BF),
            pltpu.VMEM((4, 64, 2048), BF),
            pltpu.VMEM((6, 64, 2048), BF),
            pltpu.VMEM((4, 64, 128), F32),
            pltpu.VMEM((4, 64, 128), F32),
            pltpu.VMEM((8, 4, 64, 128), BF),
            pltpu.VMEM((4, 7, 64, 128), BF),
            pltpu.VMEM((7, 2048, 128), BF),
            pltpu.VMEM((4, 64, 128), F32),
            pltpu.SemaphoreType.DMA((12,)),
            pltpu.SemaphoreType.DMA,
            pltpu.SemaphoreType.DMA((4,)),
            pltpu.SemaphoreType.DMA((7,)),
            pltpu.SemaphoreType.DMA((7,)),
        ],
        compiler_params=pltpu.CompilerParams(
            collective_id=0, has_side_effects=True, vmem_limit_bytes=60 * 1024 * 1024
        ),
    )(rhs, l_panel, x_solved, diag_inv, l_inner)


def solution(mesh):
    in_specs = (
        P(None, "row", "col"),
        P(None, "row", "col"),
        P("col", None),
        P(None, "row", None),
        P(None, "row", None),
    )
    return jax.shard_map(
        local, mesh=mesh, in_specs=in_specs, out_specs=P(None, "row", "col"), check_vma=False
    )
```

time: 175 us -> 77.9 us (0.45)
  blocking collectives: 117 us -> 0 us
  Pallas kernels: 0 us -> 76.2 us
  waiting for transfers between devices: 19.3 us -> 0 us
  matrix products: 14.8 us -> 0 us
  local copies, waits for them, and re-layouts: 13.9 us -> 1.57 us
  starting transfers between devices: 8.07 us -> 0 us
    all_to_all x6 -> x0, blocking collectives: 117 us -> none  [the longest x5 81 us: sent_to_all(): return lax.all_to_all(copies, axis, split_axis=0, concat_axis=0, tiled=True)]
    pallas_call x0 -> x1, Pallas kernels: none -> 76.2 us  [local(): pl.pallas_call(kernel, out_shape=jax.ShapeDtypeStruct((4, 64, 128), F32),...]
    all_to_all x2 -> x0, waiting for transfers between devices: 19.3 us -> none  [sent_to_all(): return lax.all_to_all(copies, axis, split_axis=0, concat_axis=0, tiled=True)]
    dot_general x11 -> x0, matrix products: 14.8 us -> none  [the longest x6 7.19 us: subtract_later(): jnp.dot(columns, segment, preferred_element_type=jnp.float32)]
    dot_general x1 -> x0, local copies, waits for them, and re-layouts: 11.4 us -> none  [local(): jnp.dot(l_panel.reshape(step_count * local_rows, solved_count), x_solved,...]
    all_to_all x2 -> x0, starting transfers between devices: 8.07 us -> none  [sent_to_all(): return lax.all_to_all(copies, axis, split_axis=0, concat_axis=0, tiled=True)]
    broadcast_in_dim x7 -> x0, local copies, waits for them, and re-layouts: 2.36 us -> none  [sent_to_all(): copies = jnp.broadcast_to(x, (lax.axis_size(axis), *x.shape))]
  transfers between devices with their start and end apart: 2 -> 0, of which waited for: 2 -> 0; matrix products, arithmetic and copies ran while one was open for 2% -> 0% of each run, Pallas kernels for 0% -> 0%
where the time goes in v1:
time: 77.9 us; the launch traced here: 77.8 us
  Pallas kernels  76.2 us (98%)
  local copies, waits for them, and re-layouts  1.57 us (2%)
    pallas_call x1, Pallas kernels, local(): pl.pallas_call(kernel, out_shape=jax.ShapeDtypeStruct((4, 64, 128), F32),...  76.2 us
    unnamed x1, local copies, waits for them, and re-layouts  1.57 us

profile of v1, /device:TPU:1, one launch (start us, length us, event | category | flops | bytes accessed | tf_op | source)
XLA Modules:
  0.0 77.8 jit_solution(8143115456488719966)
XLA Ops:
  0.0 76.2 %shard_map.55 = f32[4,64,128]{2,1,0:T(8,128)} custom-call(f32[4,64,128]{2,1,0:T(8,128)} %rhs.1, bf16[4,64,4096]{2,1,0:T(8,128)(2,1)} %panel.1, bf16[4096,1024]{1,0:T(8,128)(2,1)} %solved.1, bf16[4,64,2048]{2,1,0:T(8,128)(2,1)} %dinv.1, bf16[6,64,2048]{2,1,0:T(8,128)(2,1)} %inner.1), custom_call_target="tpu_custom_call" | custom-call | tf_op jit(solution)/shard_map/pallas_call | solution.py:155
  76.2 1.6 %copy.7 = f32[4,64,128]{2,1,0:T(8,128)} copy(f32[4,64,128]{2,1,0:T(8,128)} %shard_map.55) | data formatting | bytes 262144

commit v2 on v1

v2 whole, which is shorter than its diff:
```python
import jax
import jax.numpy as jnp
from jax import lax
from jax.experimental import pallas as pl
from jax.experimental.pallas import tpu as pltpu
from jax.sharding import PartitionSpec as P

MESH = pl.DeviceIdType.MESH
BF = jnp.bfloat16
F32 = jnp.float32


def dot(a, b):
    return jnp.dot(a, b, preferred_element_type=F32)


NEXT = (0, 2, 5)
OTHER = {(2, 0): (0, 1), (3, 0): (1, 3), (3, 1): (2, 4)}

CHIPS = sorted(
    [(dx, dy) for dx in range(4) for dy in range(4) if (dx, dy) != (0, 0)],
    key=lambda t: -(min(t[0], 4 - t[0]) + min(t[1], 4 - t[1])),
)


def local_copy(src, dst, sem):
    return pltpu.make_async_copy(src, dst, sem)


def settle(ref, sem):
    pltpu.make_async_copy(ref, ref, sem).wait()


def kernel(
    rhs, panel, solved, dinv, inner, out,
    lp, xs, dv, dq, lm, mk, lx, dx_w, rv, own, part, rs, st, ga, xout, xin, pend, pre,
    in_sem, rs_send, rs_recv, g_send, g_recv, d_send, d_recv, m_send, m_recv, w_send, w_recv,
    x_send, x_recv,
):
    r = lax.axis_index("row")
    c = lax.axis_index("col")
    k = r % 2
    p = r // 2
    y = p % 4
    x = p // 4
    home = x // 2
    mine = pl.multiple_of(1024 * k, 1024)
    other = pl.multiple_of(1024 * (1 - k), 1024)
    sib = (2 * p + 1 - k, c)
    chips = [((x + dx) % 4) * 4 + (y + dy) % 4 for dx, dy in CHIPS]

    def send(src, dst, ssem, rsem, dev):
        pltpu.make_async_remote_copy(
            src_ref=src, dst_ref=dst, send_sem=ssem, recv_sem=rsem,
            device_id=dev, device_id_type=MESH,
        ).start()

    d_load = [local_copy(dinv.at[j], dv.at[j], in_sem.at[10 + j]) for j in range(3)]
    p_load = local_copy(panel, lp, in_sem.at[0])
    x_load = []
    for i in range(4):
        for half, off in enumerate((4 + i, 3 - i)):
            dest = (c + off) % 8
            x_load.append(
                local_copy(
                    solved.at[:, pl.ds(pl.multiple_of(dest * 128, 128), 128)],
                    xs.at[i, :, pl.ds(128 * half, 128)],
                    in_sem.at[1 + 2 * i + half],
                )
            )
    d_load[0].start()
    p_load.start()
    for cp in x_load:
        cp.start()
    r_load = local_copy(rhs, rv, in_sem.at[9])
    r_load.start()
    d_load[1].start()
    d_load[2].start()
    w_load = []
    for i in range(3):
        w_load.append(local_copy(inner.at[NEXT[i]], lm.at[i, 1], in_sem.at[13 + i]))
    for i, n in OTHER.values():
        w_load.append(local_copy(inner.at[n, :, pl.ds(mine, 1024)], lx.at[i, 1], in_sem.at[16 + i]))
    for m in range(4):
        w_load.append(
            local_copy(dinv.at[m, :, pl.ds(mine, 1024)], dx_w.at[m, 1], in_sem.at[19 + m])
        )
    for cp in w_load:
        cp.start()

    barrier = pltpu.get_barrier_semaphore()
    for off in range(1, 8):
        pl.semaphore_signal(barrier, inc=1, device_id=(r, (c + off) % 8), device_id_type=MESH)
    pl.semaphore_signal(barrier, inc=1, device_id=sib, device_id_type=MESH)
    for q in chips:
        for core in range(2):
            pl.semaphore_signal(barrier, inc=1, device_id=(2 * q + core, c), device_id_type=MESH)

    slice_of = lambda core: jnp.where(core == 0, c, 15 - c)
    my_slice = slice_of(k)
    my_local = pl.multiple_of((my_slice - 8 * k) * 128, 128)

    @pl.loop(0, my_slice)
    def _(i):
        rows = pl.ds(pl.multiple_of(i * 128, 128), 128)
        for j in range(3):
            dq[j, rows, :] = jnp.zeros((128, 128), BF)

    def send_inverse(j):
        rows = pl.ds(pl.multiple_of(r * 64, 64), 64)
        for d in range(2):
            core = (k + d) % 2
            s = slice_of(core)
            src = dv.at[j, :, pl.ds(pl.multiple_of(s * 128, 128), 128)]
            dst = dq.at[j, rows]

            @pl.when(p >= s)
            def _():
                for q in chips:
                    send(src, dst, d_send.at[j], d_recv.at[j], (2 * q + core, c))
                if d == 0:
                    local_copy(src, dst, d_recv.at[j]).start()
                else:
                    send(src, dst, d_send.at[j], d_recv.at[j], sib)

    def sent_inverse(j):
        near, far = p >= slice_of(k), p >= slice_of(1 - k)
        for rows, cond in (
            (1984, near & far),
            (960, near & jnp.logical_not(far)),
            (1024, far & jnp.logical_not(near)),
        ):

            @pl.when(cond)
            def _():
                settle(dq.at[j, pl.ds(0, rows)], d_send.at[j])

    def got_inverse(j):
        for s in range(16):

            @pl.when(my_slice == s)
            def _():
                settle(dq.at[j, pl.ds(128 * s, 2048 - 128 * s)], d_recv.at[j])

    def send_weights():
        for i in range(3):
            send(inner.at[NEXT[i]], lm.at[i, 0], w_send.at[0], w_recv.at[i], sib)
        for m in range(4):
            send(dinv.at[m, :, pl.ds(other, 1024)], dx_w.at[m, 0], w_send.at[1], w_recv.at[4], sib)
        for i, n in OTHER.values():
            send(inner.at[n, :, pl.ds(other, 1024)], lx.at[i, 0], w_send.at[2], w_recv.at[3], sib)

    def make_next(i):
        got_inverse(i)
        w_load[i].wait()
        settle(lm.at[i, 0], w_recv.at[i])
        block = dot(lm[i].reshape(128, 2048), dq[i])
        cols = pl.ds(my_local, 128)
        mk[i, :, cols] = block.astype(BF)
        for off in (4, 5, 3, 6, 2, 7, 1):
            send(mk.at[i, :, cols], mk.at[i, :, cols], m_send.at[i], m_recv.at[i], (r, (c + off) % 8))

    def rs_send_one(off, m):
        send(part.at[off, m], rs.at[m, off - 1], rs_send, rs_recv.at[m], (r, (c + off) % 8))

    def rs_send_all(m):
        for off in (4, 5, 3, 6, 2, 7, 1):
            rs_send_one(off, m)

    p_load.wait()
    for i in range(4):
        x_load[2 * i].wait()
        x_load[2 * i + 1].wait()
        acc = dot(lp[...].reshape(256, 4096), xs[i]).reshape(4, 64, 256)
        part[4 + i] = acc[:, :, :128].astype(BF)
        if i < 3:
            part[3 - i] = acc[:, :, 128:].astype(BF)
        else:
            own[...] = acc[:, :, 128:]
        if i == 0:
            pl.semaphore_wait(barrier, 38)
            d_load[0].wait()
            send_inverse(0)
        rs_send_one(4 + i, 0)
        if i < 3:
            rs_send_one(3 - i, 0)
        if i == 0:
            send_weights()
    rs_send_all(1)
    d_load[1].wait()
    send_inverse(1)

    def reduce(m):
        settle(rs.at[m], rs_recv.at[m])
        total = own[m]
        for s in range(7):
            total = total + rs[m, s].astype(F32)
        return rv[m] - total

    slot = pl.ds(pl.multiple_of((r % 16) * 64, 64), 64)

    def spread(n, value):
        st[n] = value.astype(BF)
        for q in chips:
            send(st.at[n], ga.at[n, slot], g_send.at[n], g_recv.at[n], (2 * q + home, c))

        @pl.when(k == home)
        def _():
            local_copy(st.at[n], ga.at[n, slot], g_recv.at[n]).start()

        @pl.when(k != home)
        def _():
            send(st.at[n], ga.at[n, slot], g_send.at[n], g_recv.at[n], sib)

    def exchange(e, value):
        xout[e] = value
        send(xout.at[e], xin.at[e], x_send.at[e], x_recv.at[e], sib)

    def exchanged(e):
        settle(xin.at[e], x_recv.at[e])
        return xin[e]

    r_load.wait()
    spread(0, reduce(0))
    d_load[2].wait()
    make_next(0)
    send_inverse(2)
    rs_send_all(2)
    pend[1] = reduce(1)
    make_next(1)
    rs_send_all(3)
    for cp in w_load[3:]:
        cp.wait()
    settle(dx_w.at[:, 0], w_recv.at[4])
    settle(lx.at[:, 0], w_recv.at[3])

    for m in range(4):
        settle(ga.at[m], g_recv.at[m])
        if m < 3:
            settle(mk.at[m, :, pl.ds(0, 896)], m_recv.at[m])
            upd = dot(mk[m], ga[m])
            if m == 1:
                settle(ga.at[4], g_recv.at[4])
                upd = upd + dot(lx[0].reshape(128, 1024), ga[4])
            if m == 2:
                settle(ga.at[5], g_recv.at[5])
                upd = upd + dot(lx[2].reshape(128, 1024), ga[5]) + pre[...]
            exchange(m, upd[:64])
        sol = dot(dx_w[m].reshape(128, 1024), ga[m])
        exchange(3 + m, sol[:64])
        if m < 3:
            spread(m + 1, pend[m + 1] - (upd[64:] + exchanged(m)))
        cur = sol[64:] + exchanged(3 + m)
        if m < 2:
            spread(4 + m, cur)
        out[m] = cur
        if m == 0:
            pend[2] = reduce(2)
            make_next(2)
        if m == 1:
            pend[3] = reduce(3)
            pre[...] = dot(lx[1].reshape(128, 1024), ga[4])

    settle(part.at[pl.ds(1, 7)], rs_send)
    for n in range(6):
        @pl.when(k == home)
        def _():
            settle(ga.at[n, pl.ds(0, 960)], g_send.at[n])

        @pl.when(k != home)
        def _():
            settle(ga.at[n], g_send.at[n])

    for j in range(3):
        sent_inverse(j)
        settle(mk.at[j, :, pl.ds(0, 896)], m_send.at[j])
    settle(lm.at[:, 0], w_send.at[0])
    settle(dx_w.at[:, 0], w_send.at[1])
    settle(lx.at[:, 0], w_send.at[2])
    for e in range(7):
        settle(xin.at[e], x_send.at[e])


def local(rhs, l_panel, x_solved, diag_inv, l_inner):
    any_spec = pl.BlockSpec(memory_space=pl.ANY)
    dma = pltpu.SemaphoreType.DMA
    return pl.pallas_call(
        kernel,
        out_shape=jax.ShapeDtypeStruct((4, 64, 128), F32),
        in_specs=[any_spec] * 5,
        out_specs=pl.BlockSpec(memory_space=pltpu.VMEM),
        scratch_shapes=[
            pltpu.VMEM((4, 64, 4096), BF),
            pltpu.VMEM((4, 4096, 256), BF),
            pltpu.VMEM((3, 64, 2048), BF),
            pltpu.VMEM((3, 2048, 128), BF),
            pltpu.VMEM((3, 2, 64, 2048), BF),
            pltpu.VMEM((3, 128, 1024), BF),
            pltpu.VMEM((3, 2, 64, 1024), BF),
            pltpu.VMEM((4, 2, 64, 1024), BF),
            pltpu.VMEM((4, 64, 128), F32),
            pltpu.VMEM((4, 64, 128), F32),
            pltpu.VMEM((8, 4, 64, 128), BF),
            pltpu.VMEM((4, 7, 64, 128), BF),
            pltpu.VMEM((6, 64, 128), BF),
            pltpu.VMEM((6, 1024, 128), BF),
            pltpu.VMEM((7, 64, 128), F32),
            pltpu.VMEM((7, 64, 128), F32),
            pltpu.VMEM((4, 64, 128), F32),
            pltpu.VMEM((128, 128), F32),
            dma((23,)),
            dma,
            dma((4,)),
            dma((6,)),
            dma((6,)),
            dma((3,)),
            dma((3,)),
            dma((3,)),
            dma((3,)),
            dma((3,)),
            dma((5,)),
            dma((7,)),
            dma((7,)),
        ],
        compiler_params=pltpu.CompilerParams(
            collective_id=0, has_side_effects=True, vmem_limit_bytes=60 * 1024 * 1024
        ),
    )(rhs, l_panel, x_solved, diag_inv, l_inner)


def solution(mesh):
    in_specs = (
        P(None, "row", "col"),
        P(None, "row", "col"),
        P("col", None),
        P(None, "row", None),
        P(None, "row", None),
    )
    return jax.shard_map(
        local, mesh=mesh, in_specs=in_specs, out_specs=P(None, "row", "col"), check_vma=False
    )
```

time: 77.9 us -> 58.5 us (0.75)
  Pallas kernels: 76.2 us -> 56.9 us
    pallas_call x1, Pallas kernels: 76.2 us -> 56.9 us  [local(): pl.pallas_call(kernel, out_shape=jax.ShapeDtypeStruct((4, 64, 128), F32),...]
where the time goes in v2:
time: 58.5 us
  Pallas kernels  56.9 us (97%)
  local copies, waits for them, and re-layouts  1.57 us (3%)
    pallas_call x1, Pallas kernels, local(): pl.pallas_call(kernel, out_shape=jax.ShapeDtypeStruct((4, 64, 128), F32),...  56.9 us
    unnamed x1, local copies, waits for them, and re-layouts  1.57 us

profile of v2, /device:TPU:1, one launch (start us, length us, event | category | flops | bytes accessed | tf_op | source)
XLA Modules:
  0.0 58.5 jit_solution(4549025821346697978)
XLA Ops:
  0.0 56.9 %shard_map.55 = f32[4,64,128]{2,1,0:T(8,128)} custom-call(f32[4,64,128]{2,1,0:T(8,128)} %rhs.1, bf16[4,64,4096]{2,1,0:T(8,128)(2,1)} %panel.1, bf16[4096,1024]{1,0:T(8,128)(2,1)} %solved.1, bf16[4,64,2048]{2,1,0:T(8,128)(2,1)} %dinv.1, bf16[6,64,2048]{2,1,0:T(8,128)(2,1)} %inner.1), custom_call_target="tpu_custom_call" | custom-call | tf_op jit(solution)/shard_map/pallas_call | solution.py:287
  56.9 1.6 %copy.7 = f32[4,64,128]{2,1,0:T(8,128)} copy(f32[4,64,128]{2,1,0:T(8,128)} %shard_map.55) | data formatting | bytes 262144

commit v3 on v2

--- a/solution.py
+++ b/solution.py
@@ -14,8 +14,8 @@
     return jnp.dot(a, b, preferred_element_type=F32)
 
 
-NEXT = (0, 2, 5)
-OTHER = {(2, 0): (0, 1), (3, 0): (1, 3), (3, 1): (2, 4)}
+FIRST = (0, 1, 3)
+LATER = (2, 4, 5)
 
 CHIPS = sorted(
     [(dx, dy) for dx in range(4) for dy in range(4) if (dx, dy) != (0, 0)],
@@ -55,7 +55,6 @@
             device_id=dev, device_id_type=MESH,
         ).start()
 
-    d_load = [local_copy(dinv.at[j], dv.at[j], in_sem.at[10 + j]) for j in range(3)]
     p_load = local_copy(panel, lp, in_sem.at[0])
     x_load = []
     for i in range(4):
@@ -68,24 +67,26 @@
                     in_sem.at[1 + 2 * i + half],
                 )
             )
-    d_load[0].start()
-    p_load.start()
-    for cp in x_load:
-        cp.start()
     r_load = local_copy(rhs, rv, in_sem.at[9])
-    r_load.start()
-    d_load[1].start()
-    d_load[2].start()
+    d_load = [local_copy(dinv.at[1 + j], dv.at[j], in_sem.at[10 + j]) for j in range(2)]
     w_load = []
     for i in range(3):
-        w_load.append(local_copy(inner.at[NEXT[i]], lm.at[i, 1], in_sem.at[13 + i]))
-    for i, n in OTHER.values():
-        w_load.append(local_copy(inner.at[n, :, pl.ds(mine, 1024)], lx.at[i, 1], in_sem.at[16 + i]))
+        w_load.append(local_copy(inner.at[LATER[i]], lm.at[i, 1], in_sem.at[13 + i]))
+    for i in range(3):
+        w_load.append(
+            local_copy(inner.at[FIRST[i], :, pl.ds(mine, 1024)], lx.at[i, 1], in_sem.at[16 + i])
+        )
     for m in range(4):
         w_load.append(
             local_copy(dinv.at[m, :, pl.ds(mine, 1024)], dx_w.at[m, 1], in_sem.at[19 + m])
         )
-    for cp in w_load:
+    p_load.start()
+    for cp in x_load[:4]:
+        cp.start()
+    d_load[0].start()
+    for cp in x_load[4:]:
+        cp.start()
+    for cp in [r_load, d_load[1]] + w_load:
         cp.start()
 
     barrier = pltpu.get_barrier_semaphore()
@@ -103,7 +104,7 @@
     @pl.loop(0, my_slice)
     def _(i):
         rows = pl.ds(pl.multiple_of(i * 128, 128), 128)
-        for j in range(3):
+        for j in range(2):
             dq[j, rows, :] = jnp.zeros((128, 128), BF)
 
     def send_inverse(j):
@@ -143,19 +144,19 @@
                 settle(dq.at[j, pl.ds(128 * s, 2048 - 128 * s)], d_recv.at[j])
 
     def send_weights():
+        for m in range(4):
+            send(dinv.at[m, :, pl.ds(other, 1024)], dx_w.at[m, 0], w_send.at[0], w_recv.at[0], sib)
         for i in range(3):
-            send(inner.at[NEXT[i]], lm.at[i, 0], w_send.at[0], w_recv.at[i], sib)
-        for m in range(4):
-            send(dinv.at[m, :, pl.ds(other, 1024)], dx_w.at[m, 0], w_send.at[1], w_recv.at[4], sib)
-        for i, n in OTHER.values():
-            send(inner.at[n, :, pl.ds(other, 1024)], lx.at[i, 0], w_send.at[2], w_recv.at[3], sib)
-
-    def make_next(i):
-        got_inverse(i)
-        w_load[i].wait()
-        settle(lm.at[i, 0], w_recv.at[i])
-        block = dot(lm[i].reshape(128, 2048), dq[i])
-        cols = pl.ds(my_local, 128)
+            send(
+                inner.at[FIRST[i], :, pl.ds(other, 1024)], lx.at[i, 0], w_send.at[1], w_recv.at[1], sib
+            )
+        for i in range(3):
+            send(inner.at[LATER[i]], lm.at[i, 0], w_send.at[2], w_recv.at[2], sib)
+
+    cols = pl.ds(my_local, 128)
+
+    def make_product(i, j):
+        block = dot(lm[i].reshape(128, 2048), dq[j])
         mk[i, :, cols] = block.astype(BF)
         for off in (4, 5, 3, 6, 2, 7, 1):
             send(mk.at[i, :, cols], mk.at[i, :, cols], m_send.at[i], m_recv.at[i], (r, (c + off) % 8))
@@ -166,6 +167,11 @@
     def rs_send_all(m):
         for off in (4, 5, 3, 6, 2, 7, 1):
             rs_send_one(off, m)
+
+    def rs_chunk(i):
+        rs_send_one(4 + i, 0)
+        if i < 3:
+            rs_send_one(3 - i, 0)
 
     p_load.wait()
     for i in range(4):
@@ -177,18 +183,15 @@
             part[3 - i] = acc[:, :, 128:].astype(BF)
         else:
             own[...] = acc[:, :, 128:]
-        if i == 0:
+        if i == 1:
             pl.semaphore_wait(barrier, 38)
+            rs_chunk(0)
             d_load[0].wait()
             send_inverse(0)
-        rs_send_one(4 + i, 0)
-        if i < 3:
-            rs_send_one(3 - i, 0)
-        if i == 0:
-            send_weights()
+        if i >= 1:
+            rs_chunk(i)
     rs_send_all(1)
-    d_load[1].wait()
-    send_inverse(1)
+    send_weights()
 
     def reduce(m):
         settle(rs.at[m], rs_recv.at[m])
@@ -220,49 +223,69 @@
         settle(xin.at[e], x_recv.at[e])
         return xin[e]
 
+    def arrived(n):
+        settle(ga.at[n], g_recv.at[n])
+
+    def finish(m, value):
+        out[m] = value
+
+    def half(w, n):
+        return dot(w.reshape(128, 1024), ga[n])
+
     r_load.wait()
     spread(0, reduce(0))
-    d_load[2].wait()
-    make_next(0)
-    send_inverse(2)
     rs_send_all(2)
+    rs_send_all(3)
+    for cp in w_load:
+        cp.wait()
+    settle(dx_w.at[:, 0], w_recv.at[0])
+    settle(lx.at[:, 0], w_recv.at[1])
+    settle(lm.at[:, 0], w_recv.at[2])
+
+    arrived(0)
+    sol = half(dx_w[0], 0)
+    exchange(0, sol[:64])
+    sol = sol[64:] + exchanged(0)
+    spread(1, sol)
+    d_load[1].wait()
+    send_inverse(1)
+    finish(0, sol)
     pend[1] = reduce(1)
-    make_next(1)
-    rs_send_all(3)
-    for cp in w_load[3:]:
-        cp.wait()
-    settle(dx_w.at[:, 0], w_recv.at[4])
-    settle(lx.at[:, 0], w_recv.at[3])
-
-    for m in range(4):
-        settle(ga.at[m], g_recv.at[m])
-        if m < 3:
-            settle(mk.at[m, :, pl.ds(0, 896)], m_recv.at[m])
-            upd = dot(mk[m], ga[m])
-            if m == 1:
-                settle(ga.at[4], g_recv.at[4])
-                upd = upd + dot(lx[0].reshape(128, 1024), ga[4])
-            if m == 2:
-                settle(ga.at[5], g_recv.at[5])
-                upd = upd + dot(lx[2].reshape(128, 1024), ga[5]) + pre[...]
-            exchange(m, upd[:64])
-        sol = dot(dx_w[m].reshape(128, 1024), ga[m])
-        exchange(3 + m, sol[:64])
-        if m < 3:
-            spread(m + 1, pend[m + 1] - (upd[64:] + exchanged(m)))
-        cur = sol[64:] + exchanged(3 + m)
-        if m < 2:
-            spread(4 + m, cur)
-        out[m] = cur
-        if m == 0:
-            pend[2] = reduce(2)
-            make_next(2)
+    got_inverse(0)
+    make_product(0, 0)
+    make_product(1, 0)
+
+    arrived(1)
+    upd = half(lx[0], 1)
+    exchange(1, upd[:64])
+    spread(2, pend[1] - (upd[64:] + exchanged(1)))
+    pre[0] = half(lx[1], 1)
+    pre[1] = half(lx[2], 1)
+    got_inverse(1)
+    make_product(2, 1)
+    pend[2] = reduce(2)
+    pend[3] = reduce(3)
+
+    for m in (1, 2):
+        arrived(m + 1)
+        settle(mk.at[m * m - m, :, pl.ds(0, 896)], m_recv.at[m * m - m])
+        upd = dot(mk[m * m - m], ga[m + 1]) + pre[m - 1]
+        exchange(2 * m, upd[:64])
+        sol = half(dx_w[m], m + 1)
+        exchange(2 * m + 1, sol[:64])
+        spread(m + 2, pend[m + 1] - (upd[64:] + exchanged(2 * m)))
+        finish(m, sol[64:] + exchanged(2 * m + 1))
         if m == 1:
-            pend[3] = reduce(3)
-            pre[...] = dot(lx[1].reshape(128, 1024), ga[4])
+            settle(mk.at[1, :, pl.ds(0, 896)], m_recv.at[1])
+            pre[1] = pre[1] + dot(mk[1], ga[2])
+
+    arrived(4)
+    sol = half(dx_w[3], 4)
+    exchange(6, sol[:64])
+    finish(3, sol[64:] + exchanged(6))
 
     settle(part.at[pl.ds(1, 7)], rs_send)
-    for n in range(6):
+    for n in range(5):
         @pl.when(k == home)
         def _():
             settle(ga.at[n, pl.ds(0, 960)], g_send.at[n])
@@ -271,12 +294,13 @@
         def _():
             settle(ga.at[n], g_send.at[n])
 
-    for j in range(3):
+    for j in range(2):
         sent_inverse(j)
-        settle(mk.at[j, :, pl.ds(0, 896)], m_send.at[j])
-    settle(lm.at[:, 0], w_send.at[0])
-    settle(dx_w.at[:, 0], w_send.at[1])
-    settle(lx.at[:, 0], w_send.at[2])
+    for i in range(3):
+        settle(mk.at[i, :, pl.ds(0, 896)], m_send.at[i])
+    settle(dx_w.at[:, 0], w_send.at[0])
+    settle(lx.at[:, 0], w_send.at[1])
+    settle(lm.at[:, 0], w_send.at[2])
     for e in range(7):
         settle(xin.at[e], x_send.at[e])
 
@@ -286,14 +310,14 @@
     dma = pltpu.SemaphoreType.DMA
     return pl.pallas_call(
         kernel,
-        out_shape=jax.ShapeDtypeStruct((4, 64, 128), F32),
+        out_shape=pltpu.VMEM((4, 64, 128), F32),
         in_specs=[any_spec] * 5,
         out_specs=pl.BlockSpec(memory_space=pltpu.VMEM),
         scratch_shapes=[
             pltpu.VMEM((4, 64, 4096), BF),
             pltpu.VMEM((4, 4096, 256), BF),
-            pltpu.VMEM((3, 64, 2048), BF),
-            pltpu.VMEM((3, 2048, 128), BF),
+            pltpu.VMEM((2, 64, 2048), BF),
+            pltpu.VMEM((2, 2048, 128), BF),
             pltpu.VMEM((3, 2, 64, 2048), BF),
             pltpu.VMEM((3, 128, 1024), BF),
             pltpu.VMEM((3, 2, 64, 1024), BF),
@@ -302,23 +326,23 @@
             pltpu.VMEM((4, 64, 128), F32),
             pltpu.VMEM((8, 4, 64, 128), BF),
             pltpu.VMEM((4, 7, 64, 128), BF),
-            pltpu.VMEM((6, 64, 128), BF),
-            pltpu.VMEM((6, 1024, 128), BF),
+            pltpu.VMEM((5, 64, 128), BF),
+            pltpu.VMEM((5, 1024, 128), BF),
             pltpu.VMEM((7, 64, 128), F32),
             pltpu.VMEM((7, 64, 128), F32),
             pltpu.VMEM((4, 64, 128), F32),
-            pltpu.VMEM((128, 128), F32),
+            pltpu.VMEM((2, 128, 128), F32),
             dma((23,)),
             dma,
             dma((4,)),
-            dma((6,)),
-            dma((6,)),
+            dma((5,)),
+            dma((5,)),
+            dma((2,)),
+            dma((2,)),
             dma((3,)),
             dma((3,)),
             dma((3,)),
             dma((3,)),
-            dma((3,)),
-            dma((5,)),
             dma((7,)),
             dma((7,)),
         ],

time: 58.5 us -> 53.3 us (0.911)
  Pallas kernels: 56.9 us -> 52.5 us
  local copies, waits for them, and re-layouts: 1.57 us -> 0.66 us
    pallas_call x1, Pallas kernels: 56.9 us -> 52.5 us  [local(): pl.pallas_call(kernel, out_shape=pltpu.VMEM((4, 64, 128), F32), in_specs=...]
    unnamed x1, local copies, waits for them, and re-layouts: 1.57 us -> 0.66 us
where the time goes in v3:
time: 53.3 us; the launch traced here: 53.2 us
  Pallas kernels  52.5 us (98%)
  local copies, waits for them, and re-layouts  0.66 us (1%)
    pallas_call x1, Pallas kernels, local(): pl.pallas_call(kernel, out_shape=pltpu.VMEM((4, 64, 128), F32), in_specs=...  52.5 us

profile of v3, /device:TPU:1, one launch (start us, length us, event | category | flops | bytes accessed | tf_op | source)
XLA Modules:
  0.0 53.2 jit_solution(14624066873545791099)
XLA Ops:
  0.0 52.5 %shard_map.55 = f32[4,64,128]{2,1,0:T(8,128)S(1)} custom-call(f32[4,64,128]{2,1,0:T(8,128)} %rhs.1, bf16[4,64,4096]{2,1,0:T(8,128)(2,1)} %panel.1, bf16[4096,1024]{1,0:T(8,128)(2,1)} %solved.1, bf16[4,64,2048]{2,1,0:T(8,128)(2,1)} %dinv.1, bf16[6,64,2048]{2,1,0:T(8,128)(2,1)} %inner.1), custom_call_target="tpu_custom_call" | custom-call | tf_op jit(solution)/shard_map/pallas_call | solution.py:311
  52.5 0.7 %copy.7 = f32[4,64,128]{2,1,0:T(8,128)} copy(f32[4,64,128]{2,1,0:T(8,128)S(1)} %shard_map.55) | data formatting | bytes 262144

commit v4 on v3

v4 whole, which is shorter than its diff:
```python
import jax
import jax.numpy as jnp
from jax import lax
from jax.experimental import pallas as pl
from jax.experimental.pallas import tpu as pltpu
from jax.sharding import PartitionSpec as P

MESH = pl.DeviceIdType.MESH
BF = jnp.bfloat16
F32 = jnp.float32


def dot(a, b):
    return jnp.dot(a, b, preferred_element_type=F32)


FIRST = (0, 1, 3)
LATER = (2, 4, 5)

CHIPS = sorted(
    [(dx, dy) for dx in range(4) for dy in range(4) if (dx, dy) != (0, 0)],
    key=lambda t: -(min(t[0], 4 - t[0]) + min(t[1], 4 - t[1])),
)


def local_copy(src, dst, sem):
    return pltpu.make_async_copy(src, dst, sem)


def settle(ref, sem):
    pltpu.make_async_copy(ref, ref, sem).wait()


def kernel(
    rhs, panel, solved, dinv, inner, out,
    lp, xs, ds, dq, wd, wl, mk, rv, own, part, rs, st, ga, rb, xout, xin, pend, pre,
    in_sem, rs_send, rs_recv, g_send, g_recv, d_send, d_recv, m_send, m_recv, h_send, h_recv,
    w_send, w_recv, x_send, x_recv,
):
    r = lax.axis_index("row")
    c = lax.axis_index("col")
    k = r % 2
    p = r // 2
    y = p % 4
    x = p // 4
    sib = (2 * p + 1 - k, c)
    chips = [((x + dx) % 4) * 4 + (y + dy) % 4 for dx, dy in CHIPS]

    def send(src, dst, ssem, rsem, dev):
        pltpu.make_async_remote_copy(
            src_ref=src, dst_ref=dst, send_sem=ssem, recv_sem=rsem,
            device_id=dev, device_id_type=MESH,
        ).start()

    barrier = pltpu.get_barrier_semaphore()
    for off in range(1, 8):
        pl.semaphore_signal(barrier, inc=1, device_id=(r, (c + off) % 8), device_id_type=MESH)
    pl.semaphore_signal(barrier, inc=1, device_id=sib, device_id_type=MESH)
    for q in chips:
        for core in range(2):
            pl.semaphore_signal(barrier, inc=1, device_id=(2 * q + core, c), device_id_type=MESH)


    p_load = [
        local_copy(panel.at[0], lp.at[0], in_sem.at[0]),
        local_copy(panel.at[pl.ds(1, 3)], lp.at[pl.ds(1, 3)], in_sem.at[12]),
    ]
    x_load = []
    for i in range(4):
        for half, off in enumerate((4 + i, 3 - i)):
            dest = (c + off) % 8
            x_load.append(
                local_copy(
                    solved.at[:, pl.ds(pl.multiple_of(dest * 128, 128), 128)],
                    xs.at[i, :, pl.ds(128 * half, 128)],
                    in_sem.at[1 + 2 * i + half],
                )
            )
    r_load = local_copy(rhs, rv, in_sem.at[9])
    d_load = [local_copy(dinv.at[m], wd.at[m, k], in_sem.at[13 + m]) for m in range(4)]
    l_load = [
        local_copy(inner.at[pl.ds(0, 3)], wl.at[pl.ds(0, 3), k], in_sem.at[10]),
        local_copy(inner.at[pl.ds(3, 3)], wl.at[pl.ds(3, 3), k], in_sem.at[11]),
    ]
    slice_of = lambda core: jnp.where(core == 0, c, 15 - c)
    my_slice = slice_of(k)
    s_load = [
        local_copy(
            dinv.at[1 + j, :, pl.ds(pl.multiple_of(slice_of(core) * 128, 128), 128)],
            ds.at[j, core],
            in_sem.at[17 + 2 * j + core],
        )
        for j in range(2)
        for core in range(2)
    ]
    p_load[0].start()
    for cp in x_load[:4] + s_load[:2] + x_load[4:]:
        cp.start()
    for cp in [p_load[1], r_load] + s_load[2:] + d_load[:1] + l_load + d_load[1:]:
        cp.start()

    @pl.loop(0, my_slice)
    def _(i):
        rows = pl.ds(pl.multiple_of(i * 128, 128), 128)
        for j in range(2):
            dq[j, rows, :] = jnp.zeros((128, 128), BF)

    def send_inverse(j, piece):
        rows = pl.ds(pl.multiple_of(r * 64, 64), 64)
        for d in range(2):
            core = (k + d) % 2
            s = slice_of(core)
            src = ds.at[j, core]
            dst = dq.at[j, rows]

            @pl.when(p >= s)
            def _():
                for q in chips[piece::3]:
                    send(src, dst, d_send.at[j], d_recv.at[j], (2 * q + core, c))
                if piece > 0:
                    return
                if d == 0:
                    local_copy(src, dst, d_recv.at[j]).start()
                else:
                    send(src, dst, d_send.at[j], d_recv.at[j], sib)

    def sent_inverse(j):
        near, far = p >= slice_of(k), p >= slice_of(1 - k)
        for rows, cond in (
            (1984, near & far),
            (960, near & jnp.logical_not(far)),
            (1024, far & jnp.logical_not(near)),
        ):

            @pl.when(cond)
            def _():
                settle(dq.at[j, pl.ds(0, rows)], d_send.at[j])

    def got_inverse(j):
        for s in range(16):

            @pl.when(my_slice == s)
            def _():
                settle(dq.at[j, pl.ds(128 * s, 2048 - 128 * s)], d_recv.at[j])

    def send_weights():
        send(dinv.at[0], wd.at[0, k], w_send.at[0], w_recv.at[0], sib)
        send(inner.at[pl.ds(0, 3)], wl.at[pl.ds(0, 3), k], w_send.at[1], w_recv.at[1], sib)
        send(inner.at[pl.ds(3, 3)], wl.at[pl.ds(3, 3), k], w_send.at[2], w_recv.at[2], sib)
        send(dinv.at[pl.ds(1, 3)], wd.at[pl.ds(1, 3), k], w_send.at[3], w_recv.at[3], sib)

    def pass_on(i, plane, off, e):
        slot = jnp.where(k == 0, plane % 8, 15 - plane % 8)
        send(
            mk.at[i, slot], mk.at[i, slot], m_send.at[i, e], m_recv.at[i, e], (r, (c + off) % 8)
        )

    def make_product(i, n, j):
        mk[i, my_slice] = dot(wl[n].reshape(128, 2048), dq[j]).astype(BF)
        for off in (2, 6, 1, 7):
            pass_on(i, c, off, 0)

    def relay_product(i):
        settle(mk.at[i, pl.ds(0, 4)], m_recv.at[i, 0])
        far = 2 + 4 * k
        pass_on(i, c + 8 - far, far, 1)
        pass_on(i, c + 6, 1, 1)
        pass_on(i, c + 2, 7, 1)

    def share_product(i):
        settle(mk.at[i, pl.ds(0, 3)], m_recv.at[i, 1])
        part_cols = mk.at[i, pl.ds(8 * k, 8)]
        send(part_cols, part_cols, h_send.at[i], h_recv.at[i], sib)

    def got_product(i):
        settle(mk.at[i, pl.ds(0, 8)], h_recv.at[i])

    def rs_send_one(off, m):
        send(part.at[off, m], rs.at[m, off - 1], rs_send, rs_recv.at[m], (r, (c + off) % 8))

    def rs_send_all(m):
        for off in (4, 5, 3, 6, 2, 7, 1):
            rs_send_one(off, m)

    def rs_chunk(i):
        rs_send_one(4 + i, 0)
        if i < 3:
            rs_send_one(3 - i, 0)

    def product(i, lo, hi):
        rows = 64 * (hi - lo)
        acc = dot(lp[lo:hi].reshape(rows, 4096), xs[i]).reshape(hi - lo, 64, 256)
        part[4 + i, lo:hi] = acc[:, :, :128].astype(BF)
        if i < 3:
            part[3 - i, lo:hi] = acc[:, :, 128:].astype(BF)
        else:
            own[lo:hi] = acc[:, :, 128:]

    p_load[0].wait()
    for i in range(4):
        x_load[2 * i].wait()
        x_load[2 * i + 1].wait()
        product(i, 0, 1)
        if i == 0:
            pl.semaphore_wait(barrier, 38)
        rs_chunk(i)
        if i == 1:
            s_load[0].wait()
            s_load[1].wait()
            send_weights()
        if i >= 1:
            send_inverse(0, i - 1)
    p_load[1].wait()
    for i in range(4):
        product(i, 1, 4)
    rs_send_all(1)
    rs_send_all(2)

    lane = lax.broadcasted_iota(jnp.int32, (64, 128), 1)
    left = lane < 64
    stay = left == (k == 0)

    def turn_start(e, value):
        xout[e] = pltpu.roll(value, 64, 1)
        send(xout.at[e], xin.at[e], x_send.at[e], x_recv.at[e], sib)

    def turn_end(e, value):
        settle(xin.at[e], x_recv.at[e])
        return jnp.where(stay, value, xin[e])

    def turn(e, value):
        turn_start(e, value)
        return turn_end(e, value)

    def reduce(m):
        settle(rs.at[m], rs_recv.at[m])
        total = own[m]
        for s in range(7):
            total = total + rs[m, s].astype(F32)
        return rv[m] - total

    slot = pl.ds(pl.multiple_of(p * 64, 64), 64)

    def spread(n, value):
        st[n] = value.astype(BF)
        for q in chips:
            send(st.at[n], ga.at[n, slot], g_send.at[n], g_recv.at[n], (2 * q + k, c))
        local_copy(st.at[n], ga.at[n, slot], g_recv.at[n]).start()

    def arrived(n):
        settle(ga.at[n], g_recv.at[n])
        here = ga[n]
        there = pltpu.roll(here, 64, 1).reshape(16, 64, 128)
        here = here.reshape(16, 64, 128)
        rb[:, 0, :, :128] = here
        rb[:, 1, :, :128] = there
        rb[:, 0, :, 128:] = there
        rb[:, 1, :, 128:] = here

    def joined(i):
        return jnp.concatenate([mk[i, q] for q in range(16)], axis=1)

    def apply(w):
        prod = dot(w.reshape(128, 2048), rb[...].reshape(2048, 256))
        return jnp.where(left, prod[:64, :128], prod[64:, 128:])

    r_load.wait()
    spread(0, turn(0, reduce(0)))
    for cp in s_load[2:] + d_load + l_load:
        cp.wait()
    settle(wd.at[0, 0], w_recv.at[0])
    settle(wl.at[pl.ds(0, 3), 0], w_recv.at[1])
    settle(wl.at[pl.ds(3, 3), 0], w_recv.at[2])
    settle(wd.at[pl.ds(1, 3), 0], w_recv.at[3])
    got_inverse(0)
    make_product(0, LATER[0], 0)
    for piece in range(3):
        send_inverse(1, piece)
    rs_send_all(3)

    arrived(0)
    sol = apply(wd[0])
    spread(1, sol)
    turn_start(4, sol)
    make_product(1, LATER[1], 0)
    pend[1] = reduce(1)
    turn_start(1, pend[1])
    out[0] = turn_end(4, sol)
    relay_product(0)
    got_inverse(1)
    make_product(2, LATER[2], 1)

    arrived(1)
    spread(2, turn_end(1, pend[1]) - apply(wl[FIRST[0]]))
    relay_product(1)
    pend[2] = reduce(2)
    turn_start(2, pend[2])
    share_product(0)
    pre[...] = apply(wl[FIRST[2]])
    pend[2] = turn_end(2, pend[2]) - apply(wl[FIRST[1]])
    got_product(0)
    relay_product(2)

    for m in (1, 2):
        arrived(m + 1)
        spread(m + 2, pend[m + 1] - apply(joined(2 * m - 2)))
        sol = apply(wd[m])
        turn_start(4 + m, sol)
        if m == 1:
            share_product(1)
            pend[3] = reduce(3)
            turn_start(3, pend[3])
            got_product(1)
            pre[...] = pre[...] + apply(joined(1))
            share_product(2)
            pend[3] = turn_end(3, pend[3]) - pre[...]
        out[m] = turn_end(4 + m, sol)
        if m == 1:
            got_product(2)

    arrived(4)
    out[3] = turn(7, apply(wd[3]))

    settle(part.at[pl.ds(1, 7)], rs_send)
    for n in range(5):
        settle(ga.at[n, pl.ds(0, 960)], g_send.at[n])
    for j in range(2):
        sent_inverse(j)
    for i in range(3):
        settle(mk.at[i, pl.ds(0, 4)], m_send.at[i, 0])
        settle(mk.at[i, pl.ds(0, 3)], m_send.at[i, 1])
        settle(mk.at[i, pl.ds(0, 8)], h_send.at[i])
    settle(wd.at[0, 0], w_send.at[0])
    settle(wl.at[pl.ds(0, 3), 0], w_send.at[1])
    settle(wl.at[pl.ds(3, 3), 0], w_send.at[2])
    settle(wd.at[pl.ds(1, 3), 0], w_send.at[3])
    for e in range(8):
        settle(xin.at[e], x_send.at[e])


def local(rhs, l_panel, x_solved, diag_inv, l_inner):
    any_spec = pl.BlockSpec(memory_space=pl.ANY)
    dma = pltpu.SemaphoreType.DMA
    return pl.pallas_call(
        kernel,
        out_shape=pltpu.VMEM((4, 64, 128), F32),
        in_specs=[any_spec] * 5,
        out_specs=pl.BlockSpec(memory_space=pltpu.VMEM),
        scratch_shapes=[
            pltpu.VMEM((4, 64, 4096), BF),
            pltpu.VMEM((4, 4096, 256), BF),
            pltpu.VMEM((2, 2, 64, 128), BF),
            pltpu.VMEM((2, 2048, 128), BF),
            pltpu.VMEM((4, 2, 64, 2048), BF),
            pltpu.VMEM((6, 2, 64, 2048), BF),
            pltpu.VMEM((3, 16, 128, 128), BF),
            pltpu.VMEM((4, 64, 128), F32),
            pltpu.VMEM((4, 64, 128), F32),
            pltpu.VMEM((8, 4, 64, 128), BF),
            pltpu.VMEM((4, 7, 64, 128), BF),
            pltpu.VMEM((5, 64, 128), BF),
            pltpu.VMEM((5, 1024, 128), BF),
            pltpu.VMEM((16, 2, 64, 256), BF),
            pltpu.VMEM((8, 64, 128), F32),
            pltpu.VMEM((8, 64, 128), F32),
            pltpu.VMEM((4, 64, 128), F32),
            pltpu.VMEM((64, 128), F32),
            dma((21,)),
            dma,
            dma((4,)),
            dma((5,)),
            dma((5,)),
            dma((2,)),
            dma((2,)),
            dma((3, 2)),
            dma((3, 2)),
            dma((3,)),
            dma((3,)),
            dma((4,)),
            dma((4,)),
            dma((8,)),
            dma((8,)),
        ],
        compiler_params=pltpu.CompilerParams(
            collective_id=0, has_side_effects=True, vmem_limit_bytes=60 * 1024 * 1024
        ),
    )(rhs, l_panel, x_solved, diag_inv, l_inner)


def solution(mesh):
    in_specs = (
        P(None, "row", "col"),
        P(None, "row", "col"),
        P("col", None),
        P(None, "row", None),
        P(None, "row", None),
    )
    return jax.shard_map(
        local, mesh=mesh, in_specs=in_specs, out_specs=P(None, "row", "col"), check_vma=False
    )
```

time: 53.3 us -> 52.2 us (0.979)
  Pallas kernels: 52.5 us -> 51.5 us
    pallas_call x1, Pallas kernels: 52.5 us -> 51.5 us  [local(): pl.pallas_call(kernel, out_shape=pltpu.VMEM((4, 64, 128), F32), in_specs=...]
where the time goes in v4:
time: 52.2 us; the launch traced here: 52.1 us
  Pallas kernels  51.5 us (99%)
  local copies, waits for them, and re-layouts  0.66 us (1%)
    pallas_call x1, Pallas kernels, local(): pl.pallas_call(kernel, out_shape=pltpu.VMEM((4, 64, 128), F32), in_specs=...  51.5 us

profile of v4, /device:TPU:1, one launch (start us, length us, event | category | flops | bytes accessed | tf_op | source)
XLA Modules:
  0.0 52.1 jit_solution(13009393589922746393)
XLA Ops:
  0.0 51.5 %shard_map.55 = f32[4,64,128]{2,1,0:T(8,128)S(1)} custom-call(f32[4,64,128]{2,1,0:T(8,128)} %rhs.1, bf16[4,64,4096]{2,1,0:T(8,128)(2,1)} %panel.1, bf16[4096,1024]{1,0:T(8,128)(2,1)} %solved.1, bf16[4,64,2048]{2,1,0:T(8,128)(2,1)} %dinv.1, bf16[6,64,2048]{2,1,0:T(8,128)(2,1)} %inner.1), custom_call_target="tpu_custom_call" | custom-call | tf_op jit(solution)/shard_map/pallas_call | solution.py:344
  51.5 0.7 %copy.7 = f32[4,64,128]{2,1,0:T(8,128)} copy(f32[4,64,128]{2,1,0:T(8,128)S(1)} %shard_map.55) | data formatting | bytes 262144

commit v5 on v4

--- a/solution.py
+++ b/solution.py
@@ -33,8 +33,8 @@
 
 def kernel(
     rhs, panel, solved, dinv, inner, out,
-    lp, xs, ds, dq, wd, wl, mk, rv, own, part, rs, st, ga, rb, xout, xin, pend, pre,
-    in_sem, rs_send, rs_recv, g_send, g_recv, d_send, d_recv, m_send, m_recv, h_send, h_recv,
+    lp, xs, p0, z0, ds, dq, wd, wl, mk, rv, own, part, rs, st, ga, rb, xout, xin, pend, pre,
+    in_sem, p0_send, z0_recv, rs_send, rs_recv, g_send, g_recv, d_send, d_recv, m_send, m_recv, h_send, h_recv,
     w_send, w_recv, x_send, x_recv,
 ):
     r = lax.axis_index("row")
@@ -54,7 +54,8 @@
 
     barrier = pltpu.get_barrier_semaphore()
     for off in range(1, 8):
-        pl.semaphore_signal(barrier, inc=1, device_id=(r, (c + off) % 8), device_id_type=MESH)
+        for row in (r, 2 * p + 1 - k):
+            pl.semaphore_signal(barrier, inc=1, device_id=(row, (c + off) % 8), device_id_type=MESH)
     pl.semaphore_signal(barrier, inc=1, device_id=sib, device_id_type=MESH)
     for q in chips:
         for core in range(2):
@@ -96,7 +97,7 @@
     p_load[0].start()
     for cp in x_load[:4] + s_load[:2] + x_load[4:]:
         cp.start()
-    for cp in [p_load[1], r_load] + s_load[2:] + d_load[:1] + l_load + d_load[1:]:
+    for cp in [r_load, p_load[1]] + s_load[2:] + d_load[:1] + l_load + d_load[1:]:
         cp.start()
 
     @pl.loop(0, my_slice)
@@ -178,31 +179,85 @@
     def rs_send_one(off, m):
         send(part.at[off, m], rs.at[m, off - 1], rs_send, rs_recv.at[m], (r, (c + off) % 8))
 
-    def rs_send_all(m):
-        for off in (4, 5, 3, 6, 2, 7, 1):
+    def rs_send_all(m, offs=(4, 5, 3, 6, 2, 7, 1)):
+        for off in offs:
             rs_send_one(off, m)
 
-    def rs_chunk(i):
-        rs_send_one(4 + i, 0)
-        if i < 3:
-            rs_send_one(3 - i, 0)
+    lane = lax.broadcasted_iota(jnp.int32, (64, 128), 1)
+    left = lane < 64
+    stay = left == (k == 0)
 
     def product(i, lo, hi):
         rows = 64 * (hi - lo)
         acc = dot(lp[lo:hi].reshape(rows, 4096), xs[i]).reshape(hi - lo, 64, 256)
-        part[4 + i, lo:hi] = acc[:, :, :128].astype(BF)
+        return acc[:, :, :128], acc[:, :, 128:]
+
+    def product_later(i):
+        first, second = product(i, 1, 4)
+        part[4 + i, 1:] = first.astype(BF)
         if i < 3:
-            part[3 - i, lo:hi] = acc[:, :, 128:].astype(BF)
+            part[3 - i, 1:] = second.astype(BF)
         else:
-            own[lo:hi] = acc[:, :, 128:]
+            own[1:] = second
+
+    def fold(value):
+        top, low = value[0, :32], value[0, 32:]
+        return (
+            jnp.where(left[:32], top, pltpu.roll(low, 64, 1)),
+            jnp.where(left[:32], pltpu.roll(top, 64, 1), low),
+        )
+
+    def product_first(i):
+        for off, value in zip((4 + i, 3 - i), product(i, 0, 1)):
+            for core, folded in enumerate(fold(value)):
+                p0[2 * off + core] = folded.astype(BF)
+                if off == 0:
+                    xout[7 + core, :32] = folded
+
+    def rs_chunk(i):
+        for off in (4 + i, 3 - i):
+            dst = z0.at[8 * k + off]
+            if off:
+                send(p0.at[2 * off + k], dst, p0_send, z0_recv, (r, (c + off) % 8))
+            send(p0.at[2 * off + 1 - k], dst, p0_send, z0_recv, (2 * p + 1 - k, (c + off) % 8))
+
+    def reduce_first():
+        settle(z0.at[pl.ds(0, 15)], z0_recv)
+        mine = xout[7 + k, :32]
+        for off in range(1, 8):
+            mine = mine + z0[8 * k + off].astype(F32)
+        theirs = z0[8 * (1 - k)].astype(F32)
+        for off in range(1, 8):
+            theirs = theirs + z0[8 * (1 - k) + off].astype(F32)
+        first = jnp.where(k == 0, mine, theirs)
+        second = jnp.where(k == 0, theirs, mine)
+        return jnp.concatenate(
+            [
+                jnp.where(left[:32], first, pltpu.roll(second, 64, 1)),
+                jnp.where(left[:32], pltpu.roll(first, 64, 1), second),
+            ],
+            axis=0,
+        )
+
+    def turn_start(e, value):
+        xout[e] = pltpu.roll(value, 64, 1)
+        send(xout.at[e], xin.at[e], x_send.at[e], x_recv.at[e], sib)
+
+    def turn_end(e, value):
+        settle(xin.at[e], x_recv.at[e])
+        return jnp.where(stay, value, xin[e])
+
+    def turn(e, value):
+        turn_start(e, value)
+        return turn_end(e, value)
 
     p_load[0].wait()
     for i in range(4):
         x_load[2 * i].wait()
         x_load[2 * i + 1].wait()
-        product(i, 0, 1)
+        product_first(i)
         if i == 0:
-            pl.semaphore_wait(barrier, 38)
+            pl.semaphore_wait(barrier, 45)
         rs_chunk(i)
         if i == 1:
             s_load[0].wait()
@@ -210,27 +265,13 @@
             send_weights()
         if i >= 1:
             send_inverse(0, i - 1)
+    r_load.wait()
+    turn_start(0, rv[0])
     p_load[1].wait()
-    for i in range(4):
-        product(i, 1, 4)
-    rs_send_all(1)
-    rs_send_all(2)
-
-    lane = lax.broadcasted_iota(jnp.int32, (64, 128), 1)
-    left = lane < 64
-    stay = left == (k == 0)
-
-    def turn_start(e, value):
-        xout[e] = pltpu.roll(value, 64, 1)
-        send(xout.at[e], xin.at[e], x_send.at[e], x_recv.at[e], sib)
-
-    def turn_end(e, value):
-        settle(xin.at[e], x_recv.at[e])
-        return jnp.where(stay, value, xin[e])
-
-    def turn(e, value):
-        turn_start(e, value)
-        return turn_end(e, value)
+    for i in range(3):
+        product_later(i)
+    for m in (1, 2):
+        rs_send_all(m, (4, 5, 3, 6, 2, 1))
 
     def reduce(m):
         settle(rs.at[m], rs_recv.at[m])
@@ -264,8 +305,10 @@
         prod = dot(w.reshape(128, 2048), rb[...].reshape(2048, 256))
         return jnp.where(left, prod[:64, :128], prod[64:, 128:])
 
-    r_load.wait()
-    spread(0, turn(0, reduce(0)))
+    spread(0, turn_end(0, rv[0]) - reduce_first())
+    product_later(3)
+    for m in (1, 2):
+        rs_send_all(m, (7,))
     for cp in s_load[2:] + d_load + l_load:
         cp.wait()
     settle(wd.at[0, 0], w_recv.at[0])
@@ -321,7 +364,8 @@
     arrived(4)
     out[3] = turn(7, apply(wd[3]))
 
-    settle(part.at[pl.ds(1, 7)], rs_send)
+    settle(part.at[pl.ds(1, 7), pl.ds(1, 3)], rs_send)
+    settle(p0.at[pl.ds(0, 15)], p0_send)
     for n in range(5):
         settle(ga.at[n, pl.ds(0, 960)], g_send.at[n])
     for j in range(2):
@@ -349,6 +393,8 @@
         scratch_shapes=[
             pltpu.VMEM((4, 64, 4096), BF),
             pltpu.VMEM((4, 4096, 256), BF),
+            pltpu.VMEM((16, 32, 128), BF),
+            pltpu.VMEM((16, 32, 128), BF),
             pltpu.VMEM((2, 2, 64, 128), BF),
             pltpu.VMEM((2, 2048, 128), BF),
             pltpu.VMEM((4, 2, 64, 2048), BF),
@@ -361,11 +407,13 @@
             pltpu.VMEM((5, 64, 128), BF),
             pltpu.VMEM((5, 1024, 128), BF),
             pltpu.VMEM((16, 2, 64, 256), BF),
-            pltpu.VMEM((8, 64, 128), F32),
+            pltpu.VMEM((9, 64, 128), F32),
             pltpu.VMEM((8, 64, 128), F32),
             pltpu.VMEM((4, 64, 128), F32),
             pltpu.VMEM((64, 128), F32),
             dma((21,)),
+            dma,
+            dma,
             dma,
             dma((4,)),
             dma((5,)),

time: 52.2 us -> 51.2 us (0.981)
  Pallas kernels: 51.5 us -> 50.4 us
    pallas_call x1, Pallas kernels: 51.5 us -> 50.4 us  [local(): pl.pallas_call(kernel, out_shape=pltpu.VMEM((4, 64, 128), F32), in_specs=...]
where the time goes in v5:
time: 51.2 us; the launch traced here: 51.1 us
  Pallas kernels  50.4 us (98%)
  local copies, waits for them, and re-layouts  0.66 us (1%)
    pallas_call x1, Pallas kernels, local(): pl.pallas_call(kernel, out_shape=pltpu.VMEM((4, 64, 128), F32), in_specs=...  50.4 us

profile of v5, /device:TPU:1, one launch (start us, length us, event | category | flops | bytes accessed | tf_op | source)
XLA Modules:
  0.0 51.1 jit_solution(3262802723509676064)
XLA Ops:
  0.0 50.4 %shard_map.55 = f32[4,64,128]{2,1,0:T(8,128)S(1)} custom-call(f32[4,64,128]{2,1,0:T(8,128)} %rhs.1, bf16[4,64,4096]{2,1,0:T(8,128)(2,1)} %panel.1, bf16[4096,1024]{1,0:T(8,128)(2,1)} %solved.1, bf16[4,64,2048]{2,1,0:T(8,128)(2,1)} %dinv.1, bf16[6,64,2048]{2,1,0:T(8,128)(2,1)} %inner.1), custom_call_target="tpu_custom_call" | custom-call | tf_op jit(solution)/shard_map/pallas_call | solution.py:388
  50.4 0.7 %copy.7 = f32[4,64,128]{2,1,0:T(8,128)} copy(f32[4,64,128]{2,1,0:T(8,128)S(1)} %shard_map.55) | data formatting | bytes 262144

commit v6 on v5

--- a/solution.py
+++ b/solution.py
@@ -256,9 +256,11 @@
         x_load[2 * i].wait()
         x_load[2 * i + 1].wait()
         product_first(i)
-        if i == 0:
+        if i == 1:
             pl.semaphore_wait(barrier, 45)
-        rs_chunk(i)
+            rs_chunk(0)
+        if i >= 1:
+            rs_chunk(i)
         if i == 1:
             s_load[0].wait()
             s_load[1].wait()
@@ -362,7 +364,10 @@
             got_product(2)
 
     arrived(4)
-    out[3] = turn(7, apply(wd[3]))
+    sides = rb.at[:, :, :, pl.ds(pl.multiple_of(128 * (1 - k), 128), 128)]
+    turn_start(7, dot(wd[3, 1 - k], sides[...].reshape(2048, 128)))
+    sides = rb.at[:, :, :, pl.ds(pl.multiple_of(128 * k, 128), 128)]
+    out[3] = turn_end(7, dot(wd[3, k], sides[...].reshape(2048, 128)))
 
     settle(part.at[pl.ds(1, 7), pl.ds(1, 3)], rs_send)
     settle(p0.at[pl.ds(0, 15)], p0_send)

time: 51.2 us -> 50.6 us (0.988)
    pallas_call x1, Pallas kernels: 50.4 us -> 49.9 us  [local(): pl.pallas_call(kernel, out_shape=pltpu.VMEM((4, 64, 128), F32), in_specs=...]
where the time goes in v6:
time: 50.6 us; the launch traced here: 50.5 us
  Pallas kernels  49.9 us (99%)
  local copies, waits for them, and re-layouts  0.66 us (1%)
    pallas_call x1, Pallas kernels, local(): pl.pallas_call(kernel, out_shape=pltpu.VMEM((4, 64, 128), F32), in_specs=...  49.9 us

profile of v6, /device:TPU:1, one launch (start us, length us, event | category | flops | bytes accessed | tf_op | source)
XLA Modules:
  0.0 50.5 jit_solution(1345230099577817056)
XLA Ops:
  0.0 49.9 %shard_map.55 = f32[4,64,128]{2,1,0:T(8,128)S(1)} custom-call(f32[4,64,128]{2,1,0:T(8,128)} %rhs.1, bf16[4,64,4096]{2,1,0:T(8,128)(2,1)} %panel.1, bf16[4096,1024]{1,0:T(8,128)(2,1)} %solved.1, bf16[4,64,2048]{2,1,0:T(8,128)(2,1)} %dinv.1, bf16[6,64,2048]{2,1,0:T(8,128)(2,1)} %inner.1), custom_call_target="tpu_custom_call" | custom-call | tf_op jit(solution)/shard_map/pallas_call | solution.py:393
  49.9 0.7 %copy.7 = f32[4,64,128]{2,1,0:T(8,128)} copy(f32[4,64,128]{2,1,0:T(8,128)S(1)} %shard_map.55) | data formatting | bytes 262144

commit v7 on v6

--- a/solution.py
+++ b/solution.py
@@ -321,13 +321,13 @@
     make_product(0, LATER[0], 0)
     for piece in range(3):
         send_inverse(1, piece)
-    rs_send_all(3)
+    make_product(1, LATER[1], 0)
 
     arrived(0)
     sol = apply(wd[0])
     spread(1, sol)
     turn_start(4, sol)
-    make_product(1, LATER[1], 0)
+    rs_send_all(3)
     pend[1] = reduce(1)
     turn_start(1, pend[1])
     out[0] = turn_end(4, sol)

time: 50.6 us -> 50.6 us (level)
  no operation moved by 1% of the time
where the time goes in v7:
time: 50.6 us; the launch traced here: 50.5 us
  Pallas kernels  49.9 us (99%)
  local copies, waits for them, and re-layouts  0.66 us (1%)
    pallas_call x1, Pallas kernels, local(): pl.pallas_call(kernel, out_shape=pltpu.VMEM((4, 64, 128), F32), in_specs=...  49.9 us

profile of v7, /device:TPU:1, one launch (start us, length us, event | category | flops | bytes accessed | tf_op | source)
XLA Modules:
  0.0 50.5 jit_solution(422449902939288290)
XLA Ops:
  0.0 49.9 %shard_map.55 = f32[4,64,128]{2,1,0:T(8,128)S(1)} custom-call(f32[4,64,128]{2,1,0:T(8,128)} %rhs.1, bf16[4,64,4096]{2,1,0:T(8,128)(2,1)} %panel.1, bf16[4096,1024]{1,0:T(8,128)(2,1)} %solved.1, bf16[4,64,2048]{2,1,0:T(8,128)(2,1)} %dinv.1, bf16[6,64,2048]{2,1,0:T(8,128)(2,1)} %inner.1), custom_call_target="tpu_custom_call" | custom-call | tf_op jit(solution)/shard_map/pallas_call | solution.py:393
  49.9 0.7 %copy.7 = f32[4,64,128]{2,1,0:T(8,128)} copy(f32[4,64,128]{2,1,0:T(8,128)S(1)} %shard_map.55) | data formatting | bytes 262144
